TPU v7x, 128 devices: a whole 4x4x4 slice. The times are simulated.
128 devices in a mesh: slab: 16 (over x_hi, z, core), col: 8 (over x_lo, y).
Axes of the slice: x: 4 (x_hi: 2, x_lo: 2; x = x_hi * 2 + x_lo), y: 4, z: 4, core: 2. Of those that a mesh axis runs over, the one named last changes fastest.
Arguments:
- sensitivity: bfloat16 [3, 512, 65536], P(None, 'col', 'slab'), may hold values from -0.03125 to 0.03125
- residual_force: bfloat16 [3, 65536], P(None, 'slab'), may hold values from -6 to 6
- moments: float32 [6, 64, 1024], P(None, 'slab'), as said below
- zone_label: int32 [64, 1024], P('slab'), may hold values from 0 to 511, as said below
- misfit: float32 [64, 1024], P('slab'), may hold values from 0.1 to 10
Outputs:
- hessian: float32 [512, 512], P('col', 'slab')
- gradient: float32 [512], replicated
- zone_misfit: float32 [512], replicated
Inputs may be any that keep to these rules, and one draw needn't show every extreme that they name: zone_label is the box of a 8 x 8 x 8 partition of the specimen that holds the element, the in-plane box borders displaced by at most one element; every zone occurs. `moments`: each element's moment matrix is symmetric with positive diagonal, and each diagonal entry exceeds the sum of the magnitudes of the others in its row.
All inputs are finite; a program needn't handle non-finite values.
Results may differ from a plain program's by a relative error of at most 0.0003.
Values may be sent and summed in bfloat16 or wider, within the bound.
A program may use at most 128 MiB of HBM per device.

v0:
```python
import jax
import jax.numpy as jnp
from jax import lax
from jax.sharding import PartitionSpec as P

GX = 64
GY = 16
third = 1.0 / 3.0
sixth = 1.0 / 6.0


def shifted(value, axis, by):
    count = lax.axis_size(axis)
    pairs = [(i, i + by) for i in range(count) if 0 <= i + by < count]
    return lax.ppermute(value, axis, pairs)


def mix_pair(first, second):
    return (third * first + sixth * second, sixth * first + third * second)


def shift_ahead(field, step, keep):
    moved = jnp.concatenate([field[..., step:], jnp.zeros_like(field[..., :step])], axis=-1)
    if keep is None:
        return moved
    return jnp.where(keep, moved, 0.0)


def shift_behind(field, step, keep):
    moved = jnp.concatenate([jnp.zeros_like(field[..., :step]), field[..., :-step]], axis=-1)
    if keep is None:
        return moved
    return jnp.where(keep, moved, 0.0)


def apply_moments(moments, field):
    comps = [moments[k][None, :] for k in range(6)]
    first, second, last = (field[0], field[1], field[2])
    out_x = comps[0] * first + comps[3] * second + comps[4] * last
    out_y = comps[3] * first + comps[1] * second + comps[5] * last
    out_z = comps[4] * first + comps[5] * second + comps[2] * last
    return jnp.stack([out_x, out_y, out_z])


def element_layer(lower, upper, moments):
    plane = lower.shape[-1]
    pos_y = jnp.arange(plane, dtype=jnp.int32) % GY
    not_last = pos_y != GY - 1
    not_first = pos_y != 0
    mixed_z = mix_pair(lower, upper)
    results = []
    for side_z in range(2):
        field = mixed_z[side_z]
        mixed_x = mix_pair(field, shift_ahead(field, GY, None))
        values = []
        for side_x in range(2):
            layer = mixed_x[side_x]
            mixed_y = mix_pair(layer, shift_ahead(layer, 1, not_last))
            values.append([apply_moments(moments, mixed_y[side_y]) for side_y in range(2)])
        total = values[0][0]
        total = total + shift_behind(values[1][0], GY, None)
        total = total + shift_behind(values[0][1], 1, not_first)
        total = total + shift_behind(shift_behind(values[1][1], 1, not_first), GY, None)
        results.append(total)
    return (results[0], results[1])


def on_device(sensitivity, residual_force, moments, zone_label, misfit):
    cols = sensitivity.shape[1]
    layers = moments.shape[1]
    plane_size = GX * GY
    n_slab = lax.axis_size("slab")
    n_col = lax.axis_size("col")
    width = cols * n_col
    field = sensitivity.reshape(3, cols, layers, plane_size)
    above = shifted(sensitivity[:, :, :plane_size], "slab", -1)
    levels = []
    carry = None
    first_lower = None
    for level in range(layers):
        lower = field[:, :, level].astype(jnp.float32)
        if level + 1 < layers:
            upper = field[:, :, level + 1].astype(jnp.float32)
        else:
            upper = above.astype(jnp.float32)
        to_lower, to_upper = element_layer(lower, upper, moments[:, level])
        if level == 0:
            first_lower = to_lower
        else:
            levels.append((carry + to_lower).astype(jnp.bfloat16))
        carry = to_upper
    from_below = shifted(carry.astype(jnp.bfloat16), "slab", 1).astype(carry.dtype)
    levels.insert(0, (from_below + first_lower).astype(jnp.bfloat16))
    image = jnp.stack(levels, axis=2).reshape(3, cols, layers * plane_size)
    panel_rows = lax.dot_general(
        image,
        lax.all_gather(sensitivity, "col", axis=1, tiled=True),
        (((0, 2), (0, 2)), ((), ())),
        preferred_element_type=jnp.float32,
    )
    hessian = lax.psum_scatter(panel_rows, "slab", scatter_dimension=1, tiled=True)
    grad_part = lax.dot_general(
        residual_force,
        sensitivity,
        (((0, 1), (0, 2)), ((), ())),
        preferred_element_type=jnp.float32,
    )
    grad_full = lax.dynamic_update_slice_in_dim(
        jnp.zeros((width,), jnp.float32), grad_part, lax.axis_index("col") * cols, 0
    )
    elements = layers * plane_size
    share = elements // n_col
    offset = lax.axis_index("col") * share
    zone_part = lax.dynamic_slice_in_dim(zone_label.reshape(elements), offset, share, 0)
    misfit_part = lax.dynamic_slice_in_dim(misfit.reshape(elements), offset, share, 0)
    onehot = (zone_part[:, None] == jnp.arange(width, dtype=jnp.int32)[None, :]).astype(jnp.float32)
    zone_part_sum = jnp.dot(misfit_part, onehot, precision=lax.Precision.HIGHEST)
    gradient, zone_sums = lax.psum((grad_full, zone_part_sum), ("slab", "col"))
    zone_misfit = zone_sums * (width / (elements * n_slab))
    return (hessian, gradient, zone_misfit)


def solution(mesh):
    in_specs = (
        P(None, "col", "slab"),
        P(None, "slab"),
        P(None, "slab", None),
        P("slab", None),
        P("slab", None),
    )
    out_specs = (P("col", "slab"), P(), P())
    return jax.shard_map(
        on_device, mesh=mesh, in_specs=in_specs, out_specs=out_specs, check_vma=False
    )
```

profile of v0, /device:TPU:0, one launch (start us, length us, event | category | flops | bytes accessed | tf_op | source)
XLA Modules:
  0.0 330.2 jit_solution(12702796365399645540)
XLA Ops:
  9.3 1.3 collective-permute-start
  10.6 1.2 reshape.1815
  11.8 3.2 fusion.94
  19.5 1.4 fusion.96
  21.0 1.2 fusion.14
  22.2 1.3 multiply_add_fusion.41
  24.0 1.4 slice.1015
  25.4 2.3 slice.999
  27.7 1.2 slice.967
  28.9 1.2 slice.971
  30.2 161.3 %all-reduce.56 = (f32[512]{0:T(512)}, f32[512]{0:T(512)}) all-reduce(f32[512]{0:T(512)S(1)} %dynamic_update_slice.3, f32[512]{0:T(512)S(1)} %bitcast.370), channel_id=1, replica_groups=mesh['slab'=16,'col'=8] {'slab','col'}, use_global_device_ids=true, to_apply=%region_1.2 | all-reduce | flops 1024 | bytes 8192 | tf_op jit(solution)/shard_map/psum | solution.py:118
  192.8 1.5 fusion.3
  194.6 1.2 fusion.5
  196.2 2.6 multiply_add_fusion.45
  199.9 1.2 slice.1048
  201.1 1.2 slice.1052
  204.6 1.2 slice.953
  207.6 1.2 slice.987
  212.2 1.2 slice.1016
  213.4 1.2 slice.1020
  215.7 1.2 slice.1036
  216.9 5.2 %multiply_add_fusion.42 = (f32[3,64,1024]{2,1,0:T(8,128)}, f32[3,64,1024]{2,1,0:T(8,128)}, f32[3,64,1024]{2,1,0:T(8,128)S(1)}, f32[3,64,1024]{2,1,0:T(8,128)S(1)...) fusion(f32[3,64,1024]{2,1,0:T(8,128)S(1)} %get-tuple-element.43, ...), kind=kLoop, calls=%fused_computation.212 | loop fusion | flops 8257536 | bytes 18870784 | tf_op jit(solution)/shard_map/add | solution.py:19
  222.1 2.1 multiply_add_fusion.122
  225.2 5.7 %multiply_add_fusion.46 = (f32[3,64,1024]{2,1,0:T(8,128)}, f32[3,64,1024]{2,1,0:T(8,128)}, f32[3,64,1024]{2,1,0:T(8,128)}, f32[3,64,1024]{2,1,0:T(8,128)S(1)}, f...) fusion(f32[3,64,1024]{2,1,0:T(8,128)S(1)} %get-tuple-element.44, ...), kind=kLoop, calls=%fused_computation.217 | loop fusion | flops 8257536 | bytes 18870784 | tf_op jit(solution)/shard_map/add | solution.py:19
  231.0 1.3 multiply_add_fusion.98
  236.0 1.5 fusion.76
  238.3 1.8 collective-permute-start.1
  245.9 1.4 fusion.87
  247.3 1.3 fusion.86
  248.6 1.3 fusion.85
  251.0 7.1 %convolution_bitcast_fusion = f32[64,512]{0,1:T(8,128)} fusion(bf16[3,64,4096]{2,1,0:T(8,128)(2,1)S(1)} %bitcast.171, bf16[3,512,4096]{2,1,0:T(8,128)(2,1)} %all-gather.2.cloned.1.call-done), kind=kOutput, calls=%fused_computation.1 | convolution fusion | flops 805306368 | bytes 14286848 | tf_op jit(solution)/shard_map/dot_general | solution.py:95
  258.7 64.7 %reduce-scatter.2.cloned.1.call-done = f32[64,32]{0,1:T(8,128)} async-done(((f32[64,512]{0,1:T(8,128)}), f32[64,32]{0,1:T(8,128)}) %reduce-scatter.2.cloned.1.call-update) | async-done | bytes 8208 | tf_op jit(solution)/shard_map/reduce_scatter | solution.py:101
  (176 shorter events, 31.5 us)
Async XLA Ops:
  7.2 243.8 %all-gather.2.cloned.1.call-start = ((), (), s32[]{:S(2)}) async-start(), calls=%async_computation.1 | async-start | bytes 14155776 | tf_op jit(solution)/shard_map/all_gather | solution.py:97
  7.9 315.5 %reduce-scatter.2.cloned.1.call-start = ((), (), s32[]{:S(2)}) async-start(), calls=%async_computation.2 | async-start | bytes 278528 | tf_op jit(solution)/shard_map/reduce_scatter | solution.py:101
  9.3 183.5 %collective-permute-start = (bf16[3,64,1024]{2,1,0:T(8,128)(2,1)}, bf16[3,64,1024]{2,1,0:T(8,128)(2,1)}, u32[]{:S(2)}, u32[]{:S(2)}) collective-permute-start(bf16[3,64,1024]{2,1,0:T(8,128)(2,1)} %slice.768), channel_id=1, source_target_pairs={{8,0},{16,8},{24,16},{32,24},{40,32},{48,40},{56,48},{64,56},{72,6... | collective-permute-start | bytes 1179656 | tf_op jit(solution)/shard_map/ppermute | solution.py:15
  15.9 2.4 copy-start.47
  15.9 2.4 copy-start.48
  15.9 2.6 copy-start.51
  17.2 3.8 %copy-start.19 = (bf16[3,64,1,1024]{3,2,1,0:T(2,128)(2,1)S(1)}, bf16[3,64,1,1024]{3,2,1,0:T(2,128)(2,1)}, u32[]{:S(2)}) copy-start(bf16[3,64,1,1024]{3,2,1,0:T(2,128)(2,1)} %get-tuple-element.57) | copy-start | bytes 1179652
  19.1 3.1 copy-start.4
  19.1 3.1 copy-start.18
  27.7 164.5 %copy-start.45 = (f32[6,4,1024]{2,1,0:T(4,128)S(1)}, f32[6,4,1024]{2,1,0:T(4,128)}, u32[]{:S(2)}) copy-start(f32[6,4,1024]{2,1,0:T(4,128)} %param.7) | copy-start | bytes 294916
  214.6 2.3 copy-start.49
  216.9 5.2 %copy-start.25 = (f32[1,1,1024]{2,1,0:T(1,128)S(1)}, f32[1,1,1024]{2,1,0:T(1,128)}, u32[]{:S(2)}) copy-start(f32[1,1,1024]{2,1,0:T(1,128)} %get-tuple-element.188) | copy-start | bytes 12292
  216.9 5.2 %copy-start.26 = (f32[1,1,1024]{2,1,0:T(1,128)S(1)}, f32[1,1,1024]{2,1,0:T(1,128)}, u32[]{:S(2)}) copy-start(f32[1,1,1024]{2,1,0:T(1,128)} %get-tuple-element.189) | copy-start | bytes 12292
  222.1 2.1 copy-start.11
  225.2 5.7 %copy-start.29 = (f32[1,1,1024]{2,1,0:T(1,128)S(1)}, f32[1,1,1024]{2,1,0:T(1,128)}, u32[]{:S(2)}) copy-start(f32[1,1,1024]{2,1,0:T(1,128)} %get-tuple-element.179) | copy-start | bytes 12292
  225.2 5.7 %copy-start.30 = (f32[1,1,1024]{2,1,0:T(1,128)S(1)}, f32[1,1,1024]{2,1,0:T(1,128)}, u32[]{:S(2)}) copy-start(f32[1,1,1024]{2,1,0:T(1,128)} %get-tuple-element.180) | copy-start | bytes 12292
  225.2 5.7 %copy-start.31 = (f32[1,1,1024]{2,1,0:T(1,128)S(1)}, f32[1,1,1024]{2,1,0:T(1,128)}, u32[]{:S(2)}) copy-start(f32[1,1,1024]{2,1,0:T(1,128)} %get-tuple-element.181) | copy-start | bytes 12292
  225.2 5.7 %copy-start.32 = (f32[1,1,1024]{2,1,0:T(1,128)S(1)}, f32[1,1,1024]{2,1,0:T(1,128)}, u32[]{:S(2)}) copy-start(f32[1,1,1024]{2,1,0:T(1,128)} %get-tuple-element.182) | copy-start | bytes 12292
  225.2 5.7 %copy-start.33 = (f32[1,1,1024]{2,1,0:T(1,128)S(1)}, f32[1,1,1024]{2,1,0:T(1,128)}, u32[]{:S(2)}) copy-start(f32[1,1,1024]{2,1,0:T(1,128)} %get-tuple-element.183) | copy-start | bytes 12292
  225.2 5.7 %copy-start.34 = (f32[1,1,1024]{2,1,0:T(1,128)S(1)}, f32[1,1,1024]{2,1,0:T(1,128)}, u32[]{:S(2)}) copy-start(f32[1,1,1024]{2,1,0:T(1,128)} %get-tuple-element.184) | copy-start | bytes 12292
  230.9 1.6 copy-start.7
  230.9 1.6 copy-start.35
  231.0 1.6 copy-start.36
  231.0 1.6 copy-start.37
  231.0 1.6 copy-start.42
  231.0 1.6 copy-start.43
  237.6 2.6 copy-start.13
  237.6 2.6 copy-start.14
  237.6 2.6 copy-start.15
  237.6 2.6 copy-start.16
  238.3 11.5 %collective-permute-start.1 = (bf16[3,64,1024]{2,1,0:T(8,128)(2,1)S(1)}, bf16[3,64,1024]{2,1,0:T(8,128)(2,1)S(1)}, u32[]{:S(2)}, u32[]{:S(2)}) collective-permute-start(bf16[3,64,1024]{2,1,0:T(8,128)(2,1)S(1)} %fusion.81), channel_id=1, source_target_pairs={{0,8},{8,16},{16,24},{24,32},{32,40},{40,48},{48,56},{56,64},{64,7... | collective-permute-start | bytes 1179656 | tf_op jit(solution)/shard_map/ppermute | solution.py:15
  251.0 7.1 %copy-start.50 = (f32[512]{0:T(512)S(1)}, f32[512]{0:T(512)}, u32[]{:S(2)}) copy-start(f32[512]{0:T(512)} %get-tuple-element.4) | copy-start | bytes 6148
  (24 other events, 29.4 us)
Sparse Core Ops, SparseCore 0:
  9.6 134.1 all-gather.1
  258.2 65.1 reduce-scatter.1
where the time goes:
time: 331 us; the launch traced here: 330 us
  blocking collectives  161 us (49%)
  waiting for transfers between devices  65.4 us (20%)
  other arithmetic  38.8 us (12%)
  local copies, waits for them, and re-layouts  38.6 us (12%)
  between operations  14.8 us (4%)
  matrix products  8.09 us (2%)
    psum x1, blocking collectives, on_device(): gradient, zone_sums = lax.psum((grad_full, zone_part_sum), ('slab', 'col'))  161 us
    reduce_scatter x1, waiting for transfers between devices, on_device(): lax.psum_scatter(panel_rows, 'slab', scatter_dimension=1, tiled=True)  64.7 us
    slice x24, local copies, waits for them, and re-layouts, shift_ahead(): field[..., step:]  24.9 us
    add x11, other arithmetic, mix_pair(): return (third * first + sixth * second, sixth * first + third * second)  21 us
    add x32, other arithmetic, apply_moments(): out_x = comps[0] * first + comps[3] * second + comps[4] * last  8.5 us
    dot_general x1, matrix products, on_device(): lax.dot_general(image, lax.all_gather(sensitivity, 'col', axis=1, tiled=T...  7.08 us
  transfers between devices with their start and end apart: 4, of which 1 were waited for; matrix products, arithmetic and copies ran while one was open for 22% of the time, Pallas kernels for 0%

commit v1 on v0

--- a/solution.py
+++ b/solution.py
@@ -115,7 +115,7 @@
     misfit_part = lax.dynamic_slice_in_dim(misfit.reshape(elements), offset, share, 0)
     onehot = (zone_part[:, None] == jnp.arange(width, dtype=jnp.int32)[None, :]).astype(jnp.float32)
     zone_part_sum = jnp.dot(misfit_part, onehot, precision=lax.Precision.HIGHEST)
-    gradient, zone_sums = lax.psum((grad_full, zone_part_sum), ("slab", "col"))
+    gradient, zone_sums = lax.psum(lax.psum((grad_full, zone_part_sum), "col"), "slab")
     zone_misfit = zone_sums * (width / (elements * n_slab))
     return (hessian, gradient, zone_misfit)
 

time: 331 us -> 230 us (0.69)
  blocking collectives: 161 us -> 61.9 us
    psum x1 -> x2, blocking collectives: 161 us -> 61.9 us  [the longest x1 41.2 us: on_device(): lax.psum(lax.psum((grad_full, zone_part_sum), 'col'), 'slab')]
  transfers between devices with their start and end apart: 4 -> 4, of which waited for: 1 -> 1; matrix products, arithmetic and copies ran while one was open for 22% -> 32% of each run, Pallas kernels for 0% -> 0%
where the time goes in v1:
time: 230 us; the launch traced here: 229 us
  waiting for transfers between devices  64.2 us (28%)
  blocking collectives  61.9 us (27%)
  other arithmetic  38.8 us (17%)
  local copies, waits for them, and re-layouts  38.7 us (17%)
  between operations  14.8 us (6%)
  matrix products  8.1 us (4%)
  starting transfers between devices  2.8 us (1%)
    reduce_scatter x1, waiting for transfers between devices, on_device(): lax.psum_scatter(panel_rows, 'slab', scatter_dimension=1, tiled=True)  63.4 us
    psum x1, blocking collectives, on_device(): lax.psum(lax.psum((grad_full, zone_part_sum), 'col'), 'slab')  41.2 us
    slice x24, local copies, waits for them, and re-layouts, shift_ahead(): field[..., step:]  25 us
    add x11, other arithmetic, mix_pair(): return (third * first + sixth * second, sixth * first + third * second)  21 us
    psum x1, blocking collectives, on_device(): lax.psum((grad_full, zone_part_sum), 'col')  20.7 us
    add x32, other arithmetic, apply_moments(): out_x = comps[0] * first + comps[3] * second + comps[4] * last  8.51 us
    dot_general x1, matrix products, on_device(): lax.dot_general(image, lax.all_gather(sensitivity, 'col', axis=1, tiled=T...  7.09 us
    unnamed x106, local copies, waits for them, and re-layouts  6.02 us
  transfers between devices with their start and end apart: 4, of which 1 were waited for; matrix products, arithmetic and copies ran while one was open for 32% of the time, Pallas kernels for 0%

profile of v1, /device:TPU:0, one launch (start us, length us, event | category | flops | bytes accessed | tf_op | source)
XLA Modules:
  0.0 229.3 jit_solution(16675689700365335274)
XLA Ops:
  9.3 1.3 collective-permute-start
  10.6 1.2 reshape.1815
  11.8 3.2 %fusion.94 = (bf16[3,64,1,1024]{3,2,1,0:T(2,128)(2,1)}, bf16[3,64,1,1024]{3,2,1,0:T(2,128)(2,1)S(1)}, bf16[3,64,1,1024]{3,2,1,0:T(2,128)(2,1)}, bf16[3,64,1,1024]{3,2,1,0:T(2,128)(2,1)S(1)}) fusion(bf16[3,64,4,1024]{3,2,1,0:T(4,128)(2,1)S(1)} %reshape.1815), kind=kLoop, calls=%fused_computation.332 | loop fusion | bytes 3145728 | tf_op jit(solution)/shard_map/slice | solution.py:83
  19.6 1.4 fusion.96
  22.2 1.3 multiply_add_fusion.41
  24.1 1.4 slice.1015
  25.5 2.3 %slice.999 = f32[3,64,1008]{2,1,0:T(8,128)} slice(f32[3,64,1024]{2,1,0:T(8,128)} %get-tuple-element.11), slice={[0:3], [0:64], [16:1024]} | slice | bytes 1548288 | tf_op jit(solution)/shard_map/slice | solution.py:23
  28.9 1.2 slice.971
  30.3 20.7 %all-reduce.57 = (f32[512]{0:T(512)S(1)}, f32[512]{0:T(512)S(1)}) all-reduce(f32[512]{0:T(512)S(1)} %dynamic_update_slice.3, f32[512]{0:T(512)S(1)} %bitcast.370), channel_id=1, replica_groups=mesh['slab'=16,'col'=8] {'col'}, use_global_device_ids=true, to_apply=%region_1.2 | all-reduce | flops 1024 | bytes 8192 | tf_op jit(solution)/shard_map/psum | solution.py:118
  51.0 41.2 %all-reduce.56 = (f32[512]{0:T(512)}, f32[512]{0:T(512)}) all-reduce(f32[512]{0:T(512)S(1)} %get-tuple-element.5, f32[512]{0:T(512)S(1)} %get-tuple-element.6), channel_id=1, replica_groups=mesh['slab'=16,'col'=8] {'slab'}, use_global_device_ids=true, to_apply=%region_2.3 | all-reduce | flops 1024 | bytes 8192 | tf_op jit(solution)/shard_map/psum | solution.py:118
  93.5 1.5 fusion.3
  95.3 1.3 fusion.5
  96.8 2.6 %multiply_add_fusion.45 = (f32[3,64,1024]{2,1,0:T(8,128)S(1)}, f32[3,64,1024]{2,1,0:T(8,128)S(1)}, f32[3,64,1024]{2,1,0:T(8,128)S(1)}, f32[3,64,1024]{2,1,0:T(8,...) fusion(f32[3,64,1008]{2,1,0:T(8,128)S(1)} %slice.948, ...), kind=kLoop, calls=%fused_computation.216 | loop fusion | flops 8847360 | bytes 13713408 | tf_op jit(solution)/shard_map/add | solution.py:19
  100.6 1.2 slice.1048
  101.7 1.2 slice.1052
  104.1 1.2 slice.1068
  105.3 1.2 slice.953
  108.2 1.2 slice.987
  112.9 1.2 slice.1016
  114.1 1.2 slice.1020
  116.4 1.2 slice.1036
  117.6 5.2 %multiply_add_fusion.42 = (f32[3,64,1024]{2,1,0:T(8,128)}, f32[3,64,1024]{2,1,0:T(8,128)}, f32[3,64,1024]{2,1,0:T(8,128)S(1)}, f32[3,64,1024]{2,1,0:T(8,128)S(1)...) fusion(f32[3,64,1024]{2,1,0:T(8,128)S(1)} %get-tuple-element.45, ...), kind=kLoop, calls=%fused_computation.212 | loop fusion | flops 8257536 | bytes 18870784 | tf_op jit(solution)/shard_map/add | solution.py:19
  122.8 2.2 multiply_add_fusion.122
  125.9 5.7 %multiply_add_fusion.46 = (f32[3,64,1024]{2,1,0:T(8,128)}, f32[3,64,1024]{2,1,0:T(8,128)}, f32[3,64,1024]{2,1,0:T(8,128)}, f32[3,64,1024]{2,1,0:T(8,128)S(1)}, f...) fusion(f32[3,64,1024]{2,1,0:T(8,128)S(1)} %get-tuple-element.46, ...), kind=kLoop, calls=%fused_computation.217 | loop fusion | flops 8257536 | bytes 18870784 | tf_op jit(solution)/shard_map/add | solution.py:19
  131.7 1.3 multiply_add_fusion.98
  136.8 1.5 fusion.76
  139.0 1.4 collective-permute-start.1
  146.2 1.4 fusion.87
  147.6 1.3 fusion.86
  148.9 1.3 fusion.85
  151.3 7.1 %convolution_bitcast_fusion = f32[64,512]{0,1:T(8,128)} fusion(bf16[3,64,4096]{2,1,0:T(8,128)(2,1)S(1)} %bitcast.171, bf16[3,512,4096]{2,1,0:T(8,128)(2,1)} %all-gather.2.cloned.1.call-done), kind=kOutput, calls=%fused_computation.1 | convolution fusion | flops 805306368 | bytes 14286848 | tf_op jit(solution)/shard_map/dot_general | solution.py:95
  159.0 63.4 %reduce-scatter.2.cloned.1.call-done = f32[64,32]{0,1:T(8,128)} async-done(((f32[64,512]{0,1:T(8,128)}), f32[64,32]{0,1:T(8,128)}) %reduce-scatter.2.cloned.1.call-update) | async-done | bytes 8208 | tf_op jit(solution)/shard_map/reduce_scatter | solution.py:101
  (177 shorter events, 32.7 us)
Async XLA Ops:
  7.2 144.1 %all-gather.2.cloned.1.call-start = ((), (), s32[]{:S(2)}) async-start(), calls=%async_computation.1 | async-start | bytes 14155776 | tf_op jit(solution)/shard_map/all_gather | solution.py:97
  7.9 214.5 %reduce-scatter.2.cloned.1.call-start = ((), (), s32[]{:S(2)}) async-start(), calls=%async_computation.2 | async-start | bytes 278528 | tf_op jit(solution)/shard_map/reduce_scatter | solution.py:101
  9.3 84.1 %collective-permute-start = (bf16[3,64,1024]{2,1,0:T(8,128)(2,1)}, bf16[3,64,1024]{2,1,0:T(8,128)(2,1)}, u32[]{:S(2)}, u32[]{:S(2)}) collective-permute-start(bf16[3,64,1024]{2,1,0:T(8,128)(2,1)} %slice.768), channel_id=1, source_target_pairs={{8,0},{16,8},{24,16},{32,24},{40,32},{48,40},{56,48},{64,56},{72,6... | collective-permute-start | bytes 1179656 | tf_op jit(solution)/shard_map/ppermute | solution.py:15
  15.9 2.5 %copy-start.47 = (f32[4,1024]{1,0:T(4,128)S(1)}, f32[4,1024]{1,0:T(4,128)}, u32[]{:S(2)}) copy-start(f32[4,1024]{1,0:T(4,128)} %param.9) | copy-start | bytes 49156
  15.9 2.5 %copy-start.48 = (s32[4,1024]{1,0:T(4,128)S(1)}, s32[4,1024]{1,0:T(4,128)}, u32[]{:S(2)}) copy-start(s32[4,1024]{1,0:T(4,128)} %param.8) | copy-start | bytes 49156
  16.0 2.6 %copy-start.51 = (bf16[3,4096]{1,0:T(4,128)(2,1)S(1)}, bf16[3,4096]{1,0:T(4,128)(2,1)}, u32[]{:S(2)}) copy-start(bf16[3,4096]{1,0:T(4,128)(2,1)} %param.6) | copy-start | bytes 73732
  17.2 3.8 %copy-start.19 = (bf16[3,64,1,1024]{3,2,1,0:T(2,128)(2,1)S(1)}, bf16[3,64,1,1024]{3,2,1,0:T(2,128)(2,1)}, u32[]{:S(2)}) copy-start(bf16[3,64,1,1024]{3,2,1,0:T(2,128)(2,1)} %get-tuple-element.59) | copy-start | bytes 1179652
  19.1 3.1 %copy-start.4 = (f32[3,64,1024]{2,1,0:T(8,128)S(1)}, f32[3,64,1024]{2,1,0:T(8,128)}, u32[]{:S(2)}) copy-start(f32[3,64,1024]{2,1,0:T(8,128)} %copy-done.3) | copy-start | bytes 2359300
  19.1 3.1 %copy-start.18 = (f32[3,64,1008]{2,1,0:T(8,128)S(1)}, f32[3,64,1008]{2,1,0:T(8,128)}, u32[]{:S(2)}) copy-start(f32[3,64,1008]{2,1,0:T(8,128)} %slice.966) | copy-start | bytes 2322436
  27.8 65.0 %copy-start.45 = (f32[6,4,1024]{2,1,0:T(4,128)S(1)}, f32[6,4,1024]{2,1,0:T(4,128)}, u32[]{:S(2)}) copy-start(f32[6,4,1024]{2,1,0:T(4,128)} %param.7) | copy-start | bytes 294916
  115.3 2.3 %copy-start.49 = (pred[1024]{0:T(1024)(128)(4,1)S(1)}, pred[1024]{0:T(1024)(128)(4,1)}, u32[]{:S(2)}) copy-start(pred[1024]{0:T(1024)(128)(4,1)} %fusion.92) | copy-start | bytes 3076
  117.6 5.2 %copy-start.25 = (f32[1,1,1024]{2,1,0:T(1,128)S(1)}, f32[1,1,1024]{2,1,0:T(1,128)}, u32[]{:S(2)}) copy-start(f32[1,1,1024]{2,1,0:T(1,128)} %get-tuple-element.190) | copy-start | bytes 12292
  117.6 5.2 %copy-start.26 = (f32[1,1,1024]{2,1,0:T(1,128)S(1)}, f32[1,1,1024]{2,1,0:T(1,128)}, u32[]{:S(2)}) copy-start(f32[1,1,1024]{2,1,0:T(1,128)} %get-tuple-element.191) | copy-start | bytes 12292
  122.8 2.2 copy-start.11
  125.9 5.7 %copy-start.29 = (f32[1,1,1024]{2,1,0:T(1,128)S(1)}, f32[1,1,1024]{2,1,0:T(1,128)}, u32[]{:S(2)}) copy-start(f32[1,1,1024]{2,1,0:T(1,128)} %get-tuple-element.181) | copy-start | bytes 12292
  125.9 5.7 %copy-start.30 = (f32[1,1,1024]{2,1,0:T(1,128)S(1)}, f32[1,1,1024]{2,1,0:T(1,128)}, u32[]{:S(2)}) copy-start(f32[1,1,1024]{2,1,0:T(1,128)} %get-tuple-element.182) | copy-start | bytes 12292
  125.9 5.7 %copy-start.31 = (f32[1,1,1024]{2,1,0:T(1,128)S(1)}, f32[1,1,1024]{2,1,0:T(1,128)}, u32[]{:S(2)}) copy-start(f32[1,1,1024]{2,1,0:T(1,128)} %get-tuple-element.183) | copy-start | bytes 12292
  125.9 5.7 %copy-start.32 = (f32[1,1,1024]{2,1,0:T(1,128)S(1)}, f32[1,1,1024]{2,1,0:T(1,128)}, u32[]{:S(2)}) copy-start(f32[1,1,1024]{2,1,0:T(1,128)} %get-tuple-element.184) | copy-start | bytes 12292
  125.9 5.7 %copy-start.33 = (f32[1,1,1024]{2,1,0:T(1,128)S(1)}, f32[1,1,1024]{2,1,0:T(1,128)}, u32[]{:S(2)}) copy-start(f32[1,1,1024]{2,1,0:T(1,128)} %get-tuple-element.185) | copy-start | bytes 12292
  125.9 5.7 %copy-start.34 = (f32[1,1,1024]{2,1,0:T(1,128)S(1)}, f32[1,1,1024]{2,1,0:T(1,128)}, u32[]{:S(2)}) copy-start(f32[1,1,1024]{2,1,0:T(1,128)} %get-tuple-element.186) | copy-start | bytes 12292
  131.7 1.6 copy-start.7
  131.7 1.6 copy-start.35
  131.7 1.6 copy-start.36
  131.7 1.6 copy-start.37
  131.7 1.6 copy-start.42
  131.7 1.6 copy-start.43
  138.3 2.2 copy-start.13
  138.3 2.2 copy-start.14
  138.3 2.2 copy-start.15
  138.3 2.2 copy-start.16
  139.0 11.1 %collective-permute-start.1 = (bf16[3,64,1024]{2,1,0:T(8,128)(2,1)S(1)}, bf16[3,64,1024]{2,1,0:T(8,128)(2,1)S(1)}, u32[]{:S(2)}, u32[]{:S(2)}) collective-permute-start(bf16[3,64,1024]{2,1,0:T(8,128)(2,1)S(1)} %fusion.81), channel_id=1, source_target_pairs={{0,8},{8,16},{16,24},{24,32},{32,40},{40,48},{48,56},{56,64},{64,7... | collective-permute-start | bytes 1179656 | tf_op jit(solution)/shard_map/ppermute | solution.py:15
  151.3 7.1 %copy-start.50 = (f32[512]{0:T(512)S(1)}, f32[512]{0:T(512)}, u32[]{:S(2)}) copy-start(f32[512]{0:T(512)} %get-tuple-element.4) | copy-start | bytes 6148
  (24 other events, 29.4 us)
Sparse Core Ops, SparseCore 0:
  9.6 134.3 all-gather.1
  158.5 63.8 reduce-scatter.1
